TPU v7x, 128 devices: a whole 4x4x4 slice. The times are simulated.
128 devices in a mesh: row: 8 (over y, core), col: 16 (over z, x).
Axes of the slice: x: 4, y: 4, z: 4, core: 2. Of those that a mesh axis runs over, the one named last changes fastest.
Arguments:
- kernel_panel: float32 [64, 32768], P(None, ('row', 'col')), may hold values from -4 to 16, as said below
- kernel_slab: float32 [32768, 4096], P('row', 'col'), may hold values from -4 to 20, as said below
- targets: float32 [256, 32768], P(None, ('row', 'col')), may hold values from -6 to 6
Outputs:
- updated_slab: float32 [32768, 4096], P('row', 'col')
- solved_targets: float32 [256, 32768], P('col', 'row')
- panel_factor: float32 [64, 32768], P(None, ('row', 'col'))
Inputs may be any that keep to these rules, and one draw needn't show every extreme that they name: kernel_panel[:, 0:64] is symmetric and positive definite. `kernel_slab`: rows 0 to 63 equal kernel_panel[:, 32768 - 4096 : 32768]; the last 4096 rows form a symmetric matrix.
All inputs are finite; a program needn't handle non-finite values.
Results may differ from a plain program's by a relative error of at most 0.00018.
Values sent between devices are 32-bit elements; how exact they have to be, the bound alone decides.
No kernel may reach another device: no remote copies, remote signals or barrier semaphores. Data moves between devices by JAX's collectives and lax.ppermute only.
A program may use at most 64 MiB of HBM per device.

v0:
```python
import jax
import jax.numpy as jnp
from jax import lax
from jax.sharding import PartitionSpec as P


def spread(block, axis, source):
    block = jnp.where(lax.axis_index(axis) == source, block, jnp.zeros_like(block))
    return lax.psum(block, axis)


def lower_solve(factor, values):
    return jax.scipy.linalg.solve_triangular(factor, values, lower=True)


def body(kernel_panel, kernel_slab, targets):
    highest = lax.Precision.HIGHEST
    panel_width = kernel_panel.shape[0]
    row_count = lax.axis_size("row")
    row_index = lax.axis_index("row")
    flat_index = lax.axis_index(("row", "col"))
    corner_rows = jnp.concatenate([kernel_panel[:, :panel_width], targets[:, :panel_width]], 0)
    shared = spread(corner_rows, ("row", "col"), 0)
    lower_factor = jnp.linalg.cholesky(shared[:panel_width])
    panel_factor = lower_solve(lower_factor, kernel_panel)
    gathered = lax.all_gather(panel_factor, "col", axis=1, tiled=True)
    slab_factor = spread(panel_factor, "row", row_count - 1)
    product = lax.dot_general(
        gathered,
        slab_factor,
        (((0,), (0,)), ((), ())),
        precision=highest,
        preferred_element_type=jnp.float32,
    )
    update = kernel_slab - product
    head_rows = jnp.where(row_index == 0, slab_factor, update[:panel_width])
    updated_slab = jnp.concatenate([head_rows, update[panel_width:]], 0)
    solved_lead = lower_solve(lower_factor, shared[panel_width:].T).T
    result = targets - jnp.dot(
        solved_lead, panel_factor, precision=highest, preferred_element_type=jnp.float32
    )
    head_cols = jnp.where(flat_index == 0, solved_lead, result[:, :panel_width])
    result = jnp.concatenate([head_cols, result[:, panel_width:]], 1)
    solved_targets = lax.all_to_all(result, "col", split_axis=0, concat_axis=1, tiled=True)
    return (updated_slab, solved_targets, panel_factor)


def solution(mesh):
    in_specs = (P(None, ("row", "col")), P("row", "col"), P(None, ("row", "col")))
    out_specs = (P("row", "col"), P("col", "row"), P(None, ("row", "col")))
    return jax.shard_map(body, mesh=mesh, in_specs=in_specs, out_specs=out_specs, check_vma=False)
```

profile of v0, /device:TPU:0, one launch (start us, length us, event | category | flops | bytes accessed | tf_op | source)
XLA Modules:
  0.0 286.8 jit_solution(15664791899250229156)
XLA Ops:
  7.2 0.0 all-reduce.3.cloned.1.call-start
  7.2 0.8 slice.34
  8.0 0.1 copy.22
  8.1 1.1 copy.17
  9.2 0.7 maximum_select_fusion
  9.9 0.0 all-reduce.3.cloned.1.call-update
  9.9 0.0 all-reduce.5.cloned.1.call-start
  10.0 143.3 %all-reduce.3.cloned.1.call-done = f32[320,64]{0,1:T(8,128)} async-done(((f32[320,64]{0,1:T(8,128)}), f32[320,64]{0,1:T(8,128)}) %all-reduce.3.cloned.1.call-update) | async-done | bytes 81936 | tf_op jit(solution)/shard_map/psum | solution.py:9
  153.3 0.8 slice.43
  154.1 0.1 copy.18
  154.1 0.8 fusion.5
  154.9 5.8 %cholesky.18 = f32[64,64]{1,0:T(8,128)S(1)} custom-call(f32[64,64]{1,0:T(8,128)S(1)} %fusion.5), custom_call_target="Cholesky" | custom-call | tf_op jit(solution)/shard_map/jit(cholesky)/cholesky | solution.py:24
  160.8 0.6 compare_reduce_fusion
  161.4 0.7 fusion.1
  162.1 4.9 %custom-call.7 = f32[1,64,64]{1,2,0:T(8,128)S(1)} custom-call(f32[1,64,64]{2,1,0:T(8,128)S(1)} %fusion.1), custom_call_target="InvertDiagBlocksLowerTriangular" | custom-call | tf_op jit(solution)/shard_map/jit(_solve_triangular)/triangular_solve | solution.py:13
  167.0 1.8 broadcast_select_fusion
  168.8 0.0 all-reduce.5.cloned.1.call-update
  168.8 0.0 all-gather.2.cloned.1.call-start
  168.8 0.7 all-gather.2.cloned.1.call-update
  169.5 1.2 fusion
  170.7 1.3 convolution_subtract_fusion.1
  172.0 0.8 copy.20
  172.9 5.6 %all-to-all-start = ((f32[16,16,256]{2,1,0:T(8,128)}), f32[16,16,256]{2,1,0:T(8,128)S(1)}, u32[]{:S(2)}, u32[]{:S(2)}) async-start(f32[16,16,256]{2,1,0:T(8,128)} %bitcast.7), calls=%async_computation | async-start | bytes 524288 | tf_op jit(solution)/shard_map/all_to_all | solution.py:44
  178.5 8.7 %all-to-all-done = f32[16,16,256]{2,1,0:T(8,128)S(1)} async-done(((f32[16,16,256]{2,1,0:T(8,128)}), f32[16,16,256]{2,1,0:T(8,128)S(1)}, u32[]{:S(2)}, u32[]{:S(2)}) %all-to-all-start) | async-done | bytes 262176 | tf_op jit(solution)/shard_map/all_to_all | solution.py:44
  187.2 0.7 copy.23
  187.9 38.0 %all-reduce.5.cloned.1.call-done = f32[64,256]{1,0:T(8,128)} async-done(((f32[64,256]{1,0:T(8,128)}), f32[64,256]{1,0:T(8,128)}) %all-reduce.5.cloned.1.call-update) | async-done | bytes 65552 | tf_op jit(solution)/shard_map/psum | solution.py:9
  225.9 45.2 %all-gather.2.cloned.1.call-done = f32[64,4096]{1,0:T(8,128)} async-done(((f32[64,256]{1,0:T(8,128)}), f32[64,4096]{1,0:T(8,128)}) %all-gather.2.cloned.1.call-update) | async-done | bytes 1048592 | tf_op jit(solution)/shard_map/all_gather | solution.py:26
  271.1 6.0 %convolution_subtract_fusion = f32[4096,256]{1,0:T(8,128)S(1)} fusion(f32[4096,256]{1,0:T(8,128)} %param.6, f32[64,4096]{1,0:T(8,128)} %all-gather.2.cloned.1.call-done, f32[64,256]{1,0:T(8,128)} %all-reduce.5.cloned.1.call-done), kind=kOutput, calls=%fused_computation | convolution fusion | flops 806354944 | bytes 9502720 | tf_op jit(solution)/shard_map/dot_general | solution.py:28
  277.1 0.0 copy-start
  277.1 0.3 slice.45
  277.4 0.6 copy-done
  278.0 2.3 pad_maximum_fusion
  (6 shorter events, 0.1 us)
Async XLA Ops:
  7.2 146.1 %all-reduce.3.cloned.1.call-start = ((), (), s32[]{:S(2)}) async-start(), calls=%async_computation.1 | async-start | bytes 196608 | tf_op jit(solution)/shard_map/psum | solution.py:9
  9.9 216.0 %all-reduce.5.cloned.1.call-start = ((), (), s32[]{:S(2)}) async-start(), calls=%async_computation.2 | async-start | bytes 131072 | tf_op jit(solution)/shard_map/psum | solution.py:9
  168.8 102.3 %all-gather.2.cloned.1.call-start = ((), (), s32[]{:S(2)}) async-start(), calls=%async_computation.3 | async-start | bytes 1114112 | tf_op jit(solution)/shard_map/all_gather | solution.py:26
  172.9 14.3 %all-to-all-start = ((f32[16,16,256]{2,1,0:T(8,128)}), f32[16,16,256]{2,1,0:T(8,128)S(1)}, u32[]{:S(2)}, u32[]{:S(2)}) async-start(f32[16,16,256]{2,1,0:T(8,128)} %bitcast.7), calls=%async_computation | async-start | bytes 524288 | tf_op jit(solution)/shard_map/all_to_all | solution.py:44
  277.1 0.8 copy-start
Sparse Core Ops, SparseCore 0:
  13.3 139.9 all-reduce.2
  168.9 56.9 all-reduce.4
  228.6 42.4 all-gather.1
where the time goes:
time: 287 us
  waiting for transfers between devices  236 us (82%)
  other arithmetic  15.9 us (6%)
  between operations  13.9 us (5%)
  matrix products  10.2 us (4%)
  starting transfers between devices  5.75 us (2%)
  local copies, waits for them, and re-layouts  5.16 us (2%)
    psum x2, waiting for transfers between devices, spread(): return lax.psum(block, axis)  181 us
    all_gather x1, waiting for transfers between devices, body(): gathered = lax.all_gather(panel_factor, 'col', axis=1, tiled=True)  45.2 us
    all_to_all x1, waiting for transfers between devices, body(): lax.all_to_all(result, 'col', split_axis=0, concat_axis=1, tiled=True)  8.69 us
    another operation x3, other arithmetic, body(): lower_factor = jnp.linalg.cholesky(shared[:panel_width])  6.52 us
    dot_general x1, matrix products, body(): lax.dot_general(gathered, slab_factor, (((0,), (0,)), ((), ())), precisio...  6 us
  transfers between devices with their start and end apart: 4, of which 4 were waited for; matrix products, arithmetic and copies ran while one was open for 1% of the time, Pallas kernels for 0%

commit v1 on v0

--- a/solution.py
+++ b/solution.py
@@ -2,6 +2,27 @@
 import jax.numpy as jnp
 from jax import lax
 from jax.sharding import PartitionSpec as P
+
+
+def collect(array, axis, dim):
+    peers, here, extent = (lax.axis_size(axis), lax.axis_index(axis), array.shape[dim])
+    right = [(i, (i + 1) % peers) for i in range(peers)]
+    left = [(i, (i - 1) % peers) for i in range(peers)]
+    filled = jnp.zeros((*array.shape[:dim], peers * extent, *array.shape[dim + 1 :]), array.dtype)
+    filled = lax.dynamic_update_slice_in_dim(filled, array, here * extent, axis=dim)
+    from_left = from_right = array
+    halfway = peers // 2
+    for step in range(1, halfway + 1):
+        from_left = lax.ppermute(from_left, axis, right)
+        filled = lax.dynamic_update_slice_in_dim(
+            filled, from_left, (here - step) % peers * extent, axis=dim
+        )
+        if step < peers - halfway:
+            from_right = lax.ppermute(from_right, axis, left)
+            filled = lax.dynamic_update_slice_in_dim(
+                filled, from_right, (here + step) % peers * extent, axis=dim
+            )
+    return filled
 
 
 def spread(block, axis, source):
@@ -23,7 +44,7 @@
     shared = spread(corner_rows, ("row", "col"), 0)
     lower_factor = jnp.linalg.cholesky(shared[:panel_width])
     panel_factor = lower_solve(lower_factor, kernel_panel)
-    gathered = lax.all_gather(panel_factor, "col", axis=1, tiled=True)
+    gathered = collect(panel_factor, "col", 1)
     slab_factor = spread(panel_factor, "row", row_count - 1)
     product = lax.dot_general(
         gathered,

time: 287 us -> 256 us (0.89)
  waiting for transfers between devices: 236 us -> 167 us
  starting transfers between devices: 5.75 us -> 43.9 us
    all_gather x1 -> x0, waiting for transfers between devices: 45.2 us -> none  [body(): gathered = lax.all_gather(panel_factor, 'col', axis=1, tiled=True)]
    psum x2, waiting for transfers between devices: 181 us -> 143 us  [spread(): return lax.psum(block, axis)]
    ppermute x0 -> x15, starting transfers between devices: none -> 37.1 us  [the longest x7 37 us: collect(): from_right = lax.ppermute(from_right, axis, left)]
    ppermute x0 -> x15, waiting for transfers between devices: none -> 23.9 us  [the longest x8 15.4 us: collect(): from_left = lax.ppermute(from_left, axis, right)]
    all_to_all x1, waiting for transfers between devices: 8.69 us -> 0.01 us  [body(): lax.all_to_all(result, 'col', split_axis=0, concat_axis=1, tiled=True)]
  transfers between devices with their start and end apart: 4 -> 18, of which waited for: 4 -> 9; matrix products, arithmetic and copies ran while one was open for 1% -> 1% of each run, Pallas kernels for 0% -> 0%
where the time goes in v1:
time: 256 us; the launch traced here: 255 us
  waiting for transfers between devices  167 us (65%)
  starting transfers between devices  43.9 us (17%)
  other arithmetic  15.9 us (6%)
  between operations  14.6 us (6%)
  matrix products  8.68 us (3%)
  local copies, waits for them, and re-layouts  5.4 us (2%)
    psum x2, waiting for transfers between devices, spread(): return lax.psum(block, axis)  143 us
    ppermute x7, starting transfers between devices, collect(): from_right = lax.ppermute(from_right, axis, left)  37 us
    ppermute x8, waiting for transfers between devices, collect(): from_left = lax.ppermute(from_left, axis, right)  15.4 us
    ppermute x7, waiting for transfers between devices, collect(): from_right = lax.ppermute(from_right, axis, left)  8.59 us
    all_to_all x1, starting transfers between devices, body(): lax.all_to_all(result, 'col', split_axis=0, concat_axis=1, tiled=True)  6.74 us
    another operation x3, other arithmetic, body(): lower_factor = jnp.linalg.cholesky(shared[:panel_width])  6.52 us
    another operation x2, other arithmetic, lower_solve(): return jax.scipy.linalg.solve_triangular(factor, values, lower=True)  5.55 us
    dot_general x1, matrix products, body(): lax.dot_general(gathered, slab_factor, (((0,), (0,)), ((), ())), precisio...  5.32 us
  transfers between devices with their start and end apart: 18, of which 9 were waited for; matrix products, arithmetic and copies ran while one was open for 1% of the time, Pallas kernels for 0%

profile of v1, /device:TPU:0, one launch (start us, length us, event | category | flops | bytes accessed | tf_op | source)
XLA Modules:
  0.0 255.5 jit_solution(16245997599633159891)
XLA Ops:
  7.2 0.8 slice.34
  8.1 1.1 copy.17
  9.2 0.7 maximum_select_fusion
  10.3 143.0 %all-reduce.3.cloned.1.call-done = f32[320,64]{0,1:T(8,128)} async-done(((f32[320,64]{0,1:T(8,128)}), f32[320,64]{0,1:T(8,128)}) %all-reduce.3.cloned.1.call-update) | async-done | bytes 81936 | tf_op jit(solution)/shard_map/psum | solution.py:30
  153.3 0.8 slice.43
  154.1 0.8 fusion.5
  154.9 5.8 %cholesky.18 = f32[64,64]{1,0:T(8,128)S(1)} custom-call(f32[64,64]{1,0:T(8,128)S(1)} %fusion.5), custom_call_target="Cholesky" | custom-call | tf_op jit(solution)/shard_map/jit(cholesky)/cholesky | solution.py:45
  160.8 0.6 compare_reduce_fusion
  161.4 0.7 fusion.1
  162.1 4.9 %custom-call.7 = f32[1,64,64]{1,2,0:T(8,128)S(1)} custom-call(f32[1,64,64]{2,1,0:T(8,128)S(1)} %fusion.1), custom_call_target="InvertDiagBlocksLowerTriangular" | custom-call | tf_op jit(solution)/shard_map/jit(_solve_triangular)/triangular_solve | solution.py:34
  167.1 1.7 broadcast_select_fusion
  168.8 1.2 fusion
  170.5 3.2 %collective-permute-start.1 = (f32[64,256]{1,0:T(8,128)S(1)}, f32[64,256]{1,0:T(8,128)S(1)}, u32[]{:S(2)}, u32[]{:S(2)}) collective-permute-start(f32[64,256]{1,0:T(8,128)S(1)} %get-tuple-element.6), channel_id=1, source_target_pairs={{0,15},{1,0},{2,1},{3,2},{4,3},{5,4},{6,5},{7,6},{8,7},{9,8},{10,9... | collective-permute-start | bytes 196616 | tf_op jit(solution)/shard_map/ppermute | solution.py:21
  173.7 0.8 copy.20
  174.6 6.7 %all-to-all-start = ((f32[16,16,256]{2,1,0:T(8,128)}), f32[16,16,256]{2,1,0:T(8,128)S(1)}, u32[]{:S(2)}, u32[]{:S(2)}) async-start(f32[16,16,256]{2,1,0:T(8,128)} %bitcast.7), calls=%async_computation | async-start | bytes 524288 | tf_op jit(solution)/shard_map/all_to_all | solution.py:65
  181.3 5.3 %collective-permute-start.3 = (f32[64,256]{1,0:T(8,128)S(1)}, f32[64,256]{1,0:T(8,128)S(1)}, u32[]{:S(2)}, u32[]{:S(2)}) collective-permute-start(f32[64,256]{1,0:T(8,128)S(1)} %collective-permute-done.1), channel_id=1, source_target_pairs={{0,15},{1,0},{2,1},{3,2},{4,3},{5,4},{6,5},{7,6},{8,7},{9,8},{10,9... | collective-permute-start | bytes 196616 | tf_op jit(solution)/shard_map/ppermute | solution.py:21
  186.7 1.9 collective-permute-done.3
  188.6 5.7 %collective-permute-start.5 = (f32[64,256]{1,0:T(8,128)S(1)}, f32[64,256]{1,0:T(8,128)S(1)}, u32[]{:S(2)}, u32[]{:S(2)}) collective-permute-start(f32[64,256]{1,0:T(8,128)S(1)} %collective-permute-done.3), channel_id=1, source_target_pairs={{0,15},{1,0},{2,1},{3,2},{4,3},{5,4},{6,5},{7,6},{8,7},{9,8},{10,9... | collective-permute-start | bytes 196616 | tf_op jit(solution)/shard_map/ppermute | solution.py:21
  194.3 1.9 collective-permute-done.5
  196.1 5.7 %collective-permute-start.7 = (f32[64,256]{1,0:T(8,128)S(1)}, f32[64,256]{1,0:T(8,128)S(1)}, u32[]{:S(2)}, u32[]{:S(2)}) collective-permute-start(f32[64,256]{1,0:T(8,128)S(1)} %collective-permute-done.5), channel_id=1, source_target_pairs={{0,15},{1,0},{2,1},{3,2},{4,3},{5,4},{6,5},{7,6},{8,7},{9,8},{10,9... | collective-permute-start | bytes 196616 | tf_op jit(solution)/shard_map/ppermute | solution.py:21
  201.9 0.7 copy.23
  202.6 1.1 collective-permute-done.7
  203.7 5.7 %collective-permute-start.9 = (f32[64,256]{1,0:T(8,128)S(1)}, f32[64,256]{1,0:T(8,128)S(1)}, u32[]{:S(2)}, u32[]{:S(2)}) collective-permute-start(f32[64,256]{1,0:T(8,128)S(1)} %collective-permute-done.7), channel_id=1, source_target_pairs={{0,15},{1,0},{2,1},{3,2},{4,3},{5,4},{6,5},{7,6},{8,7},{9,8},{10,9... | collective-permute-start | bytes 196616 | tf_op jit(solution)/shard_map/ppermute | solution.py:21
  209.5 1.9 collective-permute-done.9
  211.3 5.7 %collective-permute-start.11 = (f32[64,256]{1,0:T(8,128)S(1)}, f32[64,256]{1,0:T(8,128)S(1)}, u32[]{:S(2)}, u32[]{:S(2)}) collective-permute-start(f32[64,256]{1,0:T(8,128)S(1)} %collective-permute-done.9), channel_id=1, source_target_pairs={{0,15},{1,0},{2,1},{3,2},{4,3},{5,4},{6,5},{7,6},{8,7},{9,8},{10,9... | collective-permute-start | bytes 196616 | tf_op jit(solution)/shard_map/ppermute | solution.py:21
  217.3 1.8 collective-permute-done.11
  219.1 5.8 %collective-permute-start.13 = (f32[64,256]{1,0:T(8,128)S(1)}, f32[64,256]{1,0:T(8,128)S(1)}, u32[]{:S(2)}, u32[]{:S(2)}) collective-permute-start(f32[64,256]{1,0:T(8,128)S(1)} %collective-permute-done.11), channel_id=1, source_target_pairs={{0,15},{1,0},{2,1},{3,2},{4,3},{5,4},{6,5},{7,6},{8,7},{9,8},{10,9... | collective-permute-start | bytes 196616 | tf_op jit(solution)/shard_map/ppermute | solution.py:21
  225.0 7.5 %collective-permute-done.12 = f32[64,256]{1,0:T(8,128)S(1)} collective-permute-done((f32[64,256]{1,0:T(8,128)S(1)}, f32[64,256]{1,0:T(8,128)S(1)}, u32[]{:S(2)}, u32[]{:S(2)}) %collective-permute-start.12) | collective-permute-done | bytes 65568 | tf_op jit(solution)/shard_map/ppermute | solution.py:16
  232.6 7.5 %collective-permute-done.14 = f32[64,256]{1,0:T(8,128)S(1)} collective-permute-done((f32[64,256]{1,0:T(8,128)S(1)}, f32[64,256]{1,0:T(8,128)S(1)}, u32[]{:S(2)}, u32[]{:S(2)}) %collective-permute-start.14) | collective-permute-done | bytes 65568 | tf_op jit(solution)/shard_map/ppermute | solution.py:16
  240.2 5.3 %convolution_subtract_fusion = f32[4096,256]{1,0:T(8,128)S(1)} fusion(f32[4096,256]{1,0:T(8,128)} %param.6, f32[64,4096]{1,0:T(8,128)S(1)} %constant_dynamic-update-slice_fusion, f32[64,256]{1,0:T(8,128)} %all-reduce.5.cloned.1.call-done), kind=kOutput, calls=%fused_computation | convolution fusion | flops 806354944 | bytes 9502720 | tf_op jit(solution)/shard_map/dot_general | solution.py:49
  245.8 0.6 copy-done
  246.3 2.3 pad_maximum_fusion
  (51 shorter events, 1.6 us)
Async XLA Ops:
  7.2 146.1 %all-reduce.3.cloned.1.call-start = ((), (), s32[]{:S(2)}) async-start(), calls=%async_computation.1 | async-start | bytes 196608 | tf_op jit(solution)/shard_map/psum | solution.py:30
  9.9 230.2 %all-reduce.5.cloned.1.call-start = ((), (), s32[]{:S(2)}) async-start(), calls=%async_computation.2 | async-start | bytes 131072 | tf_op jit(solution)/shard_map/psum | solution.py:30
  168.8 76.7 %copy-start.1 = (f32[64,256]{1,0:T(8,128)}, f32[64,256]{1,0:T(8,128)S(1)}, u32[]{:S(2)}) copy-start(f32[64,256]{1,0:T(8,128)S(1)} %get-tuple-element.6) | copy-start | bytes 196612
  170.5 10.8 %collective-permute-start.1 = (f32[64,256]{1,0:T(8,128)S(1)}, f32[64,256]{1,0:T(8,128)S(1)}, u32[]{:S(2)}, u32[]{:S(2)}) collective-permute-start(f32[64,256]{1,0:T(8,128)S(1)} %get-tuple-element.6), channel_id=1, source_target_pairs={{0,15},{1,0},{2,1},{3,2},{4,3},{5,4},{6,5},{7,6},{8,7},{9,8},{10,9... | collective-permute-start | bytes 196616 | tf_op jit(solution)/shard_map/ppermute | solution.py:21
  173.7 13.0 %collective-permute-start = (f32[64,256]{1,0:T(8,128)S(1)}, f32[64,256]{1,0:T(8,128)S(1)}, u32[]{:S(2)}, u32[]{:S(2)}) collective-permute-start(f32[64,256]{1,0:T(8,128)S(1)} %get-tuple-element.6), channel_id=1, source_target_pairs={{0,1},{1,2},{2,3},{3,4},{4,5},{5,6},{6,7},{7,8},{8,9},{9,10},{10,1... | collective-permute-start | bytes 196616 | tf_op jit(solution)/shard_map/ppermute | solution.py:16
  174.6 27.3 %all-to-all-start = ((f32[16,16,256]{2,1,0:T(8,128)}), f32[16,16,256]{2,1,0:T(8,128)S(1)}, u32[]{:S(2)}, u32[]{:S(2)}) async-start(f32[16,16,256]{2,1,0:T(8,128)} %bitcast.7), calls=%async_computation | async-start | bytes 524288 | tf_op jit(solution)/shard_map/all_to_all | solution.py:65
  181.3 7.2 %collective-permute-start.3 = (f32[64,256]{1,0:T(8,128)S(1)}, f32[64,256]{1,0:T(8,128)S(1)}, u32[]{:S(2)}, u32[]{:S(2)}) collective-permute-start(f32[64,256]{1,0:T(8,128)S(1)} %collective-permute-done.1), channel_id=1, source_target_pairs={{0,15},{1,0},{2,1},{3,2},{4,3},{5,4},{6,5},{7,6},{8,7},{9,8},{10,9... | collective-permute-start | bytes 196616 | tf_op jit(solution)/shard_map/ppermute | solution.py:21
  186.7 7.6 %collective-permute-start.2 = (f32[64,256]{1,0:T(8,128)S(1)}, f32[64,256]{1,0:T(8,128)S(1)}, u32[]{:S(2)}, u32[]{:S(2)}) collective-permute-start(f32[64,256]{1,0:T(8,128)S(1)} %collective-permute-done), channel_id=1, source_target_pairs={{0,1},{1,2},{2,3},{3,4},{4,5},{5,6},{6,7},{7,8},{8,9},{9,10},{10,1... | collective-permute-start | bytes 196616 | tf_op jit(solution)/shard_map/ppermute | solution.py:16
  188.6 7.6 %collective-permute-start.5 = (f32[64,256]{1,0:T(8,128)S(1)}, f32[64,256]{1,0:T(8,128)S(1)}, u32[]{:S(2)}, u32[]{:S(2)}) collective-permute-start(f32[64,256]{1,0:T(8,128)S(1)} %collective-permute-done.3), channel_id=1, source_target_pairs={{0,15},{1,0},{2,1},{3,2},{4,3},{5,4},{6,5},{7,6},{8,7},{9,8},{10,9... | collective-permute-start | bytes 196616 | tf_op jit(solution)/shard_map/ppermute | solution.py:21
  194.2 7.6 %collective-permute-start.4 = (f32[64,256]{1,0:T(8,128)S(1)}, f32[64,256]{1,0:T(8,128)S(1)}, u32[]{:S(2)}, u32[]{:S(2)}) collective-permute-start(f32[64,256]{1,0:T(8,128)S(1)} %collective-permute-done.2), channel_id=1, source_target_pairs={{0,1},{1,2},{2,3},{3,4},{4,5},{5,6},{6,7},{7,8},{8,9},{9,10},{10,1... | collective-permute-start | bytes 196616 | tf_op jit(solution)/shard_map/ppermute | solution.py:16
  196.1 7.6 %collective-permute-start.7 = (f32[64,256]{1,0:T(8,128)S(1)}, f32[64,256]{1,0:T(8,128)S(1)}, u32[]{:S(2)}, u32[]{:S(2)}) collective-permute-start(f32[64,256]{1,0:T(8,128)S(1)} %collective-permute-done.5), channel_id=1, source_target_pairs={{0,15},{1,0},{2,1},{3,2},{4,3},{5,4},{6,5},{7,6},{8,7},{9,8},{10,9... | collective-permute-start | bytes 196616 | tf_op jit(solution)/shard_map/ppermute | solution.py:21
  201.8 7.6 %collective-permute-start.6 = (f32[64,256]{1,0:T(8,128)S(1)}, f32[64,256]{1,0:T(8,128)S(1)}, u32[]{:S(2)}, u32[]{:S(2)}) collective-permute-start(f32[64,256]{1,0:T(8,128)S(1)} %collective-permute-done.4), channel_id=1, source_target_pairs={{0,1},{1,2},{2,3},{3,4},{4,5},{5,6},{6,7},{7,8},{8,9},{9,10},{10,1... | collective-permute-start | bytes 196616 | tf_op jit(solution)/shard_map/ppermute | solution.py:16
  203.7 7.6 %collective-permute-start.9 = (f32[64,256]{1,0:T(8,128)S(1)}, f32[64,256]{1,0:T(8,128)S(1)}, u32[]{:S(2)}, u32[]{:S(2)}) collective-permute-start(f32[64,256]{1,0:T(8,128)S(1)} %collective-permute-done.7), channel_id=1, source_target_pairs={{0,15},{1,0},{2,1},{3,2},{4,3},{5,4},{6,5},{7,6},{8,7},{9,8},{10,9... | collective-permute-start | bytes 196616 | tf_op jit(solution)/shard_map/ppermute | solution.py:21
  209.4 7.8 %collective-permute-start.8 = (f32[64,256]{1,0:T(8,128)S(1)}, f32[64,256]{1,0:T(8,128)S(1)}, u32[]{:S(2)}, u32[]{:S(2)}) collective-permute-start(f32[64,256]{1,0:T(8,128)S(1)} %collective-permute-done.6), channel_id=1, source_target_pairs={{0,1},{1,2},{2,3},{3,4},{4,5},{5,6},{6,7},{7,8},{8,9},{9,10},{10,1... | collective-permute-start | bytes 196616 | tf_op jit(solution)/shard_map/ppermute | solution.py:16
  211.3 7.8 %collective-permute-start.11 = (f32[64,256]{1,0:T(8,128)S(1)}, f32[64,256]{1,0:T(8,128)S(1)}, u32[]{:S(2)}, u32[]{:S(2)}) collective-permute-start(f32[64,256]{1,0:T(8,128)S(1)} %collective-permute-done.9), channel_id=1, source_target_pairs={{0,15},{1,0},{2,1},{3,2},{4,3},{5,4},{6,5},{7,6},{8,7},{9,8},{10,9... | collective-permute-start | bytes 196616 | tf_op jit(solution)/shard_map/ppermute | solution.py:21
  217.3 7.7 %collective-permute-start.10 = (f32[64,256]{1,0:T(8,128)S(1)}, f32[64,256]{1,0:T(8,128)S(1)}, u32[]{:S(2)}, u32[]{:S(2)}) collective-permute-start(f32[64,256]{1,0:T(8,128)S(1)} %collective-permute-done.8), channel_id=1, source_target_pairs={{0,1},{1,2},{2,3},{3,4},{4,5},{5,6},{6,7},{7,8},{8,9},{9,10},{10,1... | collective-permute-start | bytes 196616 | tf_op jit(solution)/shard_map/ppermute | solution.py:16
  219.1 13.4 %collective-permute-start.13 = (f32[64,256]{1,0:T(8,128)S(1)}, f32[64,256]{1,0:T(8,128)S(1)}, u32[]{:S(2)}, u32[]{:S(2)}) collective-permute-start(f32[64,256]{1,0:T(8,128)S(1)} %collective-permute-done.11), channel_id=1, source_target_pairs={{0,15},{1,0},{2,1},{3,2},{4,3},{5,4},{6,5},{7,6},{8,7},{9,8},{10,9... | collective-permute-start | bytes 196616 | tf_op jit(solution)/shard_map/ppermute | solution.py:21
  224.9 7.6 %collective-permute-start.12 = (f32[64,256]{1,0:T(8,128)S(1)}, f32[64,256]{1,0:T(8,128)S(1)}, u32[]{:S(2)}, u32[]{:S(2)}) collective-permute-start(f32[64,256]{1,0:T(8,128)S(1)} %collective-permute-done.10), channel_id=1, source_target_pairs={{0,1},{1,2},{2,3},{3,4},{4,5},{5,6},{6,7},{7,8},{8,9},{9,10},{10,1... | collective-permute-start | bytes 196616 | tf_op jit(solution)/shard_map/ppermute | solution.py:16
  232.5 7.6 %collective-permute-start.14 = (f32[64,256]{1,0:T(8,128)S(1)}, f32[64,256]{1,0:T(8,128)S(1)}, u32[]{:S(2)}, u32[]{:S(2)}) collective-permute-start(f32[64,256]{1,0:T(8,128)S(1)} %collective-permute-done.12), channel_id=1, source_target_pairs={{0,1},{1,2},{2,3},{3,4},{4,5},{5,6},{6,7},{7,8},{8,9},{9,10},{10,1... | collective-permute-start | bytes 196616 | tf_op jit(solution)/shard_map/ppermute | solution.py:16
  245.5 0.8 copy-start
Sparse Core Ops, SparseCore 0:
  13.3 139.9 all-reduce.2
  174.7 58.4 all-reduce.4
